TPU v7x, 256 devices: a whole 4x4x8 slice. The times are simulated.
256 devices in a mesh: ep: 32 (over z, y), tp: 8 (over x, core).
Axes of the slice: x: 4, y: 4, z: 8, core: 2. Of those that a mesh axis runs over, the one named last changes fastest.
Arguments:
- tokens: bfloat16 [1024, 6144], P('ep', 'tp'), may hold values from -6 to 6
- expert_ids: int32 [1024, 2], P('ep'), may hold values from 0 to 7, all different within a row; in each aligned block of 32 rows (0 to 31, 32 to 63, ...) at most 16 rows name the same one
- combine_weights: float32 [1024, 2], P('ep'), may hold values from 0.1 to 1
- gate_codes: bfloat16 [6144, 65536], P(None, ('ep', 'tp')), may hold values from -6 to 6, as said below
- gate_scales: bfloat16 [192, 65536], P(None, ('ep', 'tp')), as said below
- up_codes: bfloat16 [6144, 65536], P(None, ('ep', 'tp')), may hold values from -6 to 6, as said below
- up_scales: bfloat16 [192, 65536], P(None, ('ep', 'tp')), as said below
- down_codes: bfloat16 [65536, 6144], P(('ep', 'tp')), may hold values from -6 to 6, as said below
- down_scales: bfloat16 [2048, 6144], P(('ep', 'tp')), as said below
Outputs:
- mixed: bfloat16 [1024, 6144], P('ep', 'tp')
Inputs may be any that keep to these rules, and one draw needn't show every extreme that they name: `expert_ids`: each token names 2 different experts. Among the 32 tokens of one index of ep no expert is named more than 16 times, a bound that some block reaches. `gate_codes`: every entry is one of 0, 0.5, 1, 1.5, 2, 3, 4, 6 or its negative. `up_codes`: every entry is one of 0, 0.5, 1, 1.5, 2, 3, 4, 6 or its negative. `down_codes`: every entry is one of 0, 0.5, 1, 1.5, 2, 3, 4, 6 or its negative. `gate_scales`: every entry is a power of two. `up_scales`: every entry is a power of two. `down_scales`: every entry is a power of two.
All inputs are finite; a program needn't handle non-finite values.
Results may differ from a plain program's by a relative error of at most 0.014.
Values may be sent and summed in bfloat16 or wider, within the bound.
A program may use at most 128 MiB of HBM per device.

v0:
```python
import jax
import jax.numpy as jnp
from jax import lax
from jax.sharding import PartitionSpec as P

EXPERTS = 8
CAP = 16


def dequant(code_values, scales):
    count_in, count_out = code_values.shape
    blocks = code_values.reshape(count_in // 32, 32, count_out) * scales[:, None, :]
    return blocks.reshape(count_in, count_out)


def slot_targets(expert_ids):
    count_tokens, count_top = expert_ids.shape
    flat_ids = expert_ids.reshape(-1)
    is_expert = (flat_ids[:, None] == jnp.arange(EXPERTS, dtype=jnp.int32)[None, :]).astype(
        jnp.int32
    )
    before = jnp.cumsum(is_expert, axis=0) - is_expert
    slot_rank = jnp.sum(before * is_expert, axis=1)
    return (flat_ids * CAP + slot_rank).reshape(count_tokens, count_top)


def per_device(
    tokens,
    expert_ids,
    combine_weights,
    gate_codes,
    gate_scales,
    up_codes,
    up_scales,
    down_codes,
    down_scales,
):
    owners = lax.axis_size("ep") // EXPERTS
    gate_matrix = dequant(gate_codes, gate_scales)
    up_matrix = dequant(up_codes, up_scales)
    down_matrix = dequant(down_codes, down_scales)
    target = slot_targets(expert_ids)
    slot_index = jnp.arange(EXPERTS * CAP, dtype=jnp.int32)
    chosen = jnp.zeros((EXPERTS * CAP, target.shape[0]), jnp.float32)
    weighting = jnp.zeros((target.shape[0], EXPERTS * CAP), jnp.float32)
    for column in range(target.shape[1]):
        match_rows = target[:, column][:, None] == slot_index[None, :]
        weighting = weighting + combine_weights[:, column][:, None] * match_rows.astype(jnp.float32)
        chosen = chosen + jnp.transpose(match_rows).astype(jnp.float32)
    chosen = chosen.astype(jnp.bfloat16)
    packed = jnp.dot(chosen, tokens, preferred_element_type=jnp.float32).astype(jnp.bfloat16)
    packed = packed.reshape(EXPERTS, CAP, tokens.shape[1])
    slot_rows = lax.all_gather(
        lax.all_to_all(
            jnp.repeat(packed, owners, axis=0), "ep", split_axis=0, concat_axis=0, tiled=True
        ),
        "tp",
        axis=2,
        tiled=True,
    )
    count_src, count_slots, model_width = slot_rows.shape
    flat_rows = slot_rows.reshape(count_src * count_slots, model_width)
    gate_proj = jnp.dot(flat_rows, gate_matrix, preferred_element_type=jnp.float32)
    up_proj = jnp.dot(flat_rows, up_matrix, preferred_element_type=jnp.float32)
    hidden = (jax.nn.silu(gate_proj) * up_proj).astype(jnp.bfloat16)
    partial_value = jnp.dot(hidden, down_matrix, preferred_element_type=jnp.float32).astype(
        jnp.bfloat16
    )
    partial_value = partial_value.reshape(count_src, count_slots, model_width)
    reduced = lax.psum_scatter(
        partial_value.astype(jnp.float32).astype(jnp.bfloat16),
        "tp",
        scatter_dimension=2,
        tiled=True,
    ).astype(jnp.float32)
    returned = lax.all_to_all(
        reduced.astype(jnp.bfloat16), "ep", split_axis=0, concat_axis=0, tiled=True
    ).astype(reduced.dtype)
    feature_width = returned.shape[2]
    grouped = returned.reshape(EXPERTS, owners, CAP, feature_width)
    per_expert = jnp.sum(grouped, axis=1).reshape(EXPERTS * CAP, feature_width)
    mixed_out = jnp.dot(weighting, per_expert, preferred_element_type=jnp.float32)
    return mixed_out.astype(jnp.bfloat16)


def solution(mesh):
    placed = (
        P("ep", "tp"),
        P("ep", None),
        P("ep", None),
        P(None, ("ep", "tp")),
        P(None, ("ep", "tp")),
        P(None, ("ep", "tp")),
        P(None, ("ep", "tp")),
        P(("ep", "tp"), None),
        P(("ep", "tp"), None),
    )
    return jax.shard_map(
        per_device, mesh=mesh, in_specs=placed, out_specs=P("ep", "tp"), check_vma=False
    )
```

profile of v0, /device:TPU:8, one launch (start us, length us, event | category | flops | bytes accessed | tf_op | source)
XLA Modules:
  0.0 188.0 jit_solution(12755171529070535130)
XLA Ops:
  6.5 0.0 copy-start
  6.5 0.0 copy-start.1
  6.5 0.0 copy-start.4
  6.5 0.0 all-gather.2.cloned.1.call-start
  6.5 0.9 copy.16
  7.5 0.1 eq.59
  7.6 0.1 fusion.9
  7.6 0.1 reduce_window_sum.11
  7.7 0.2 select_reduce_fusion
  7.9 0.1 reduce_sum.21
  8.0 0.1 copy.17
  8.1 0.7 multiply_add_fusion
  8.8 0.0 copy-done
  8.8 0.2 convolution_convert_fusion.1
  9.0 0.1 broadcast_in_dim.2
  9.1 34.1 %all_to_all.10 = bf16[32,16,768]{2,1,0:T(8,128)(2,1)} all-to-all(bf16[32,16,768]{2,1,0:T(8,128)(2,1)S(1)} %bitcast.30), channel_id=1, replica_groups=mesh['ep'=32,'tp'=8] {'ep'}, dimensions={0} | all-to-all | bytes 1572864 | tf_op jit(solution)/shard_map/all_to_all | solution.py:54
  43.1 0.0 all-gather.2.cloned.1.call-update
  43.2 0.0 copy-start.5
  43.2 0.0 reduce-scatter.2.cloned.1.call-start
  43.2 0.0 copy-done.1
  43.2 0.0 copy-done.4
  43.2 0.0 copy-start.2
  43.2 1.9 %bitcast_multiply_fusion.2 = bf16[6144,256]{1,0:T(8,128)(2,1)} fusion(bf16[6144,256]{1,0:T(8,128)(2,1)S(1)} %copy-done.1, bf16[192,256]{1,0:T(8,128)(2,1)S(1)} %copy-done.4), kind=kLoop, calls=%fused_computation.3 | loop fusion | flops 1572864 | bytes 6389760 | tf_op jit(solution)/shard_map/mul | solution.py:12
  45.2 0.0 copy-done.5
  45.2 1.1 copy-done.2
  46.3 0.0 copy-start.3
  46.3 0.0 copy-start.6
  46.3 0.3 bitcast_multiply_fusion
  46.6 1.6 copy-done.3
  48.2 0.0 copy-done.6
  48.2 1.9 %bitcast_multiply_fusion.1 = bf16[6144,256]{1,0:T(8,128)(2,1)} fusion(bf16[6144,256]{1,0:T(8,128)(2,1)S(1)} %copy-done.3, bf16[192,256]{1,0:T(8,128)(2,1)S(1)} %copy-done.6), kind=kLoop, calls=%fused_computation.2 | loop fusion | flops 1572864 | bytes 6389760 | tf_op jit(solution)/shard_map/mul | solution.py:12
  50.1 33.4 %all-gather.2.cloned.1.call-done = bf16[32,16,6144]{2,1,0:T(8,128)(2,1)} async-done(((bf16[32,16,768]{2,1,0:T(8,128)(2,1)}), bf16[32,16,6144]{2,1,0:T(8,128)(2,1)}) %all-gather.2.cloned.1.call-update) | async-done | bytes 6291472 | tf_op jit(solution)/shard_map/all_gather | solution.py:53
  83.4 6.3 %fusion.20 = f32[512,256]{1,0:T(8,128)} fusion(bf16[512,6144]{1,0:T(8,128)(2,1)} %bitcast.33, bf16[6144,256]{1,0:T(8,128)(2,1)} %bitcast_multiply_fusion.2), kind=kOutput, calls=%fused_computation.40 | convolution fusion | flops 1610612736 | bytes 9961472 | tf_op jit(solution)/shard_map/dot_general | solution.py:63
  89.7 13.1 %convolution_convert_fusion = bf16[512,6144]{1,0:T(8,128)(2,1)} fusion(bf16[256,6144]{1,0:T(8,128)(2,1)S(1)} %bitcast_multiply_fusion, bf16[512,6144]{1,0:T(8,128)(2,1)} %bitcast.34, bf16[6144,256]{1,0:T(8,128)(2,1)} %bitcast_multiply_fusion.1, f32[512,256]{1,0:T(8,128)} %fusion.20), kind=kOutput, calls=%fused_computation | convolution fusion | flops 3225157632 | bytes 19398656 | tf_op jit(solution)/shard_map/dot_general | solution.py:66
  102.8 0.0 copy-start.7
  102.8 0.0 reduce-scatter.2.cloned.1.call-update
  102.8 45.3 %reduce-scatter.2.cloned.1.call-done = bf16[32,16,768]{2,1,0:T(8,128)(2,1)} async-done(((bf16[32,16,6144]{2,1,0:T(8,128)(2,1)}), bf16[32,16,768]{2,1,0:T(8,128)(2,1)}) %reduce-scatter.2.cloned.1.call-update) | async-done | bytes 786448 | tf_op jit(solution)/shard_map/reduce_scatter | solution.py:70
  148.1 10.2 %all-to-all-start.1 = ((bf16[32,16,768]{2,1,0:T(8,128)(2,1)}), bf16[32,16,768]{2,1,0:T(8,128)(2,1)S(1)}, u32[]{:S(2)}, u32[]{:S(2)}) async-start(bf16[32,16,768]{2,1,0:T(8,128)(2,1)} %reduce-scatter.2.cloned.1.call-done), calls=%async_computation.2 | async-start | bytes 1572864 | tf_op jit(solution)/shard_map/all_to_all | solution.py:76
  158.3 0.0 copy-done.7
  158.3 21.9 %all-to-all-done.1 = bf16[32,16,768]{2,1,0:T(8,128)(2,1)S(1)} async-done(((bf16[32,16,768]{2,1,0:T(8,128)(2,1)}), bf16[32,16,768]{2,1,0:T(8,128)(2,1)S(1)}, u32[]{:S(2)}, u32[]{:S(2)}) %all-to-all-start.1) | async-done | bytes 786464 | tf_op jit(solution)/shard_map/all_to_all | solution.py:76
  180.2 0.1 convert_reduce_fusion
  180.3 0.8 convolution_convert_fusion.2
  (2 shorter events, 0.0 us)
Async XLA Ops:
  6.5 2.3 %copy-start = (bf16[32,768]{1,0:T(8,128)(2,1)S(1)}, bf16[32,768]{1,0:T(8,128)(2,1)}, u32[]{:S(2)}) copy-start(bf16[32,768]{1,0:T(8,128)(2,1)} %param.9) | copy-start | bytes 147460
  6.5 36.7 %copy-start.1 = (bf16[6144,256]{1,0:T(8,128)(2,1)S(1)}, bf16[6144,256]{1,0:T(8,128)(2,1)}, u32[]{:S(2)}) copy-start(bf16[6144,256]{1,0:T(8,128)(2,1)} %param.12) | copy-start | bytes 9437188
  6.5 36.7 %copy-start.4 = (bf16[192,256]{1,0:T(8,128)(2,1)S(1)}, bf16[192,256]{1,0:T(8,128)(2,1)}, u32[]{:S(2)}) copy-start(bf16[192,256]{1,0:T(8,128)(2,1)} %param.13) | copy-start | bytes 294916
  6.5 76.9 %all-gather.2.cloned.1.call-start = ((), (), s32[]{:S(2)}) async-start(), calls=%async_computation.3 | async-start | bytes 7077888 | tf_op jit(solution)/shard_map/all_gather | solution.py:53
  43.2 2.0 %copy-start.5 = (bf16[8,6144]{1,0:T(8,128)(2,1)S(1)}, bf16[8,6144]{1,0:T(8,128)(2,1)}, u32[]{:S(2)}) copy-start(bf16[8,6144]{1,0:T(8,128)(2,1)} %param.17) | copy-start | bytes 294916
  43.2 104.9 %reduce-scatter.2.cloned.1.call-start = ((), (), s32[]{:S(2)}) async-start(), calls=%async_computation.4 | async-start | bytes 7077888 | tf_op jit(solution)/shard_map/reduce_scatter | solution.py:70
  43.2 3.0 %copy-start.2 = (bf16[256,6144]{1,0:T(8,128)(2,1)S(1)}, bf16[256,6144]{1,0:T(8,128)(2,1)}, u32[]{:S(2)}) copy-start(bf16[256,6144]{1,0:T(8,128)(2,1)} %param.16) | copy-start | bytes 9437188
  46.3 1.9 %copy-start.3 = (bf16[6144,256]{1,0:T(8,128)(2,1)S(1)}, bf16[6144,256]{1,0:T(8,128)(2,1)}, u32[]{:S(2)}) copy-start(bf16[6144,256]{1,0:T(8,128)(2,1)} %param.14) | copy-start | bytes 9437188
  46.3 1.9 %copy-start.6 = (bf16[192,256]{1,0:T(8,128)(2,1)S(1)}, bf16[192,256]{1,0:T(8,128)(2,1)}, u32[]{:S(2)}) copy-start(bf16[192,256]{1,0:T(8,128)(2,1)} %param.15) | copy-start | bytes 294916
  102.8 55.5 %copy-start.7 = (f32[32,2]{0,1:T(2,128)S(1)}, f32[32,2]{0,1:T(2,128)}, u32[]{:S(2)}) copy-start(f32[32,2]{0,1:T(2,128)} %param.11) | copy-start | bytes 772
  148.1 32.1 %all-to-all-start.1 = ((bf16[32,16,768]{2,1,0:T(8,128)(2,1)}), bf16[32,16,768]{2,1,0:T(8,128)(2,1)S(1)}, u32[]{:S(2)}, u32[]{:S(2)}) async-start(bf16[32,16,768]{2,1,0:T(8,128)(2,1)} %reduce-scatter.2.cloned.1.call-done), calls=%async_computation.2 | async-start | bytes 1572864 | tf_op jit(solution)/shard_map/all_to_all | solution.py:76
Sparse Core Ops, SparseCore 0:
  43.3 40.1 all-gather.1
  102.9 45.1 reduce-scatter.1
where the time goes:
time: 188 us
  waiting for transfers between devices  101 us (54%)
  blocking collectives  34.1 us (18%)
  matrix products  20.4 us (11%)
  between operations  13.5 us (7%)
  starting transfers between devices  10.2 us (5%)
  other arithmetic  5.26 us (3%)
  local copies, waits for them, and re-layouts  3.99 us (2%)
    reduce_scatter x1, waiting for transfers between devices, per_device(): lax.psum_scatter(partial_value.astype(jnp.float32).astype(jnp.bfloat16),...  45.3 us
    all_to_all x1, blocking collectives, per_device(): lax.all_to_all(jnp.repeat(packed, owners, axis=0), 'ep', split_axis=0, co...  34.1 us
    all_gather x1, waiting for transfers between devices, per_device(): lax.all_gather(lax.all_to_all(jnp.repeat(packed, owners, axis=0), 'ep', s...  33.4 us
    all_to_all x1, waiting for transfers between devices, per_device(): lax.all_to_all(reduced.astype(jnp.bfloat16), 'ep', split_axis=0, concat_a...  21.9 us
    dot_general x1, matrix products, per_device(): jnp.dot(hidden, down_matrix, preferred_element_type=jnp.float32)  13.1 us
    all_to_all x1, starting transfers between devices, per_device(): lax.all_to_all(reduced.astype(jnp.bfloat16), 'ep', split_axis=0, concat_a...  10.2 us
    dot_general x1, matrix products, per_device(): jnp.dot(flat_rows, gate_matrix, preferred_element_type=jnp.float32)  6.3 us
    mul x3, other arithmetic, dequant(): code_values.reshape(count_in // 32, 32, count_out) * scales[:, None, :]  4.1 us
  transfers between devices with their start and end apart: 3, of which 3 were waited for; matrix products, arithmetic and copies ran while one was open for 2% of the time, Pallas kernels for 0%

commit v1 on v0

--- a/solution.py
+++ b/solution.py
@@ -50,13 +50,13 @@
     chosen = chosen.astype(jnp.bfloat16)
     packed = jnp.dot(chosen, tokens, preferred_element_type=jnp.float32).astype(jnp.bfloat16)
     packed = packed.reshape(EXPERTS, CAP, tokens.shape[1])
-    slot_rows = lax.all_gather(
-        lax.all_to_all(
-            jnp.repeat(packed, owners, axis=0), "ep", split_axis=0, concat_axis=0, tiled=True
-        ),
-        "tp",
-        axis=2,
-        tiled=True,
+    value = lax.all_to_all(
+        jnp.repeat(packed, owners, axis=0), "ep", split_axis=0, concat_axis=0, tiled=True
+    )
+    size = lax.axis_size("tp")
+    repeats = [size if d == 2 else 1 for d in range(value.ndim)]
+    slot_rows = lax.all_to_all(
+        jnp.tile(value, repeats), "tp", split_axis=2, concat_axis=2, tiled=True
     )
     count_src, count_slots, model_width = slot_rows.shape
     flat_rows = slot_rows.reshape(count_src * count_slots, model_width)

time: 188 us -> 309 us (1.64)
  local copies, waits for them, and re-layouts: 3.99 us -> 91.9 us
  waiting for transfers between devices: 101 us -> 127 us
  starting transfers between devices: 10.2 us -> 15.4 us
    all_to_all x0 -> x1, waiting for transfers between devices: none -> 65.1 us  [per_device(): lax.all_to_all(jnp.tile(value, repeats), 'tp', split_axis=2, concat_axis=...]
    unnamed x17 -> x21, local copies, waits for them, and re-layouts: 3.64 us -> 47 us
    all_to_all x0 -> x2, local copies, waits for them, and re-layouts: none -> 34.2 us  [the longest x1 28.9 us: per_device(): lax.all_to_all(jnp.tile(value, repeats), 'tp', split_axis=2, concat_axis=...]
    all_gather x1 -> x0, waiting for transfers between devices: 33.4 us -> none  [per_device(): lax.all_gather(lax.all_to_all(jnp.repeat(packed, owners, axis=0), 'ep', s...]
    another operation x0 -> x1, local copies, waits for them, and re-layouts: none -> 10.4 us  [per_device(): jnp.tile(value, repeats)]
    reduce_scatter x1, waiting for transfers between devices: 45.3 us -> 40.1 us  [per_device(): lax.psum_scatter(partial_value.astype(jnp.float32).astype(jnp.bfloat16),...]
    all_to_all x0 -> x1, starting transfers between devices: none -> 5.07 us  [per_device(): lax.all_to_all(jnp.tile(value, repeats), 'tp', split_axis=2, concat_axis=...]
  transfers between devices with their start and end apart: 3 -> 3, of which waited for: 3 -> 3; matrix products, arithmetic and copies ran while one was open for 2% -> 1% of each run, Pallas kernels for 0% -> 0%
where the time goes in v1:
time: 309 us; the launch traced here: 308 us
  waiting for transfers between devices  127 us (41%)
  local copies, waits for them, and re-layouts  91.9 us (30%)
  blocking collectives  34.1 us (11%)
  matrix products  20.4 us (7%)
  starting transfers between devices  15.4 us (5%)
  between operations  13.5 us (4%)
  other arithmetic  5.21 us (2%)
    all_to_all x1, waiting for transfers between devices, per_device(): lax.all_to_all(jnp.tile(value, repeats), 'tp', split_axis=2, concat_axis=...  65.1 us
    unnamed x21, local copies, waits for them, and re-layouts  47 us
    reduce_scatter x1, waiting for transfers between devices, per_device(): lax.psum_scatter(partial_value.astype(jnp.float32).astype(jnp.bfloat16),...  40.1 us
    all_to_all x1, blocking collectives, per_device(): lax.all_to_all(jnp.repeat(packed, owners, axis=0), 'ep', split_axis=0, co...  34.1 us
    all_to_all x1, local copies, waits for them, and re-layouts, per_device(): lax.all_to_all(jnp.tile(value, repeats), 'tp', split_axis=2, concat_axis=...  28.9 us
    all_to_all x1, waiting for transfers between devices, per_device(): lax.all_to_all(reduced.astype(jnp.bfloat16), 'ep', split_axis=0, concat_a...  21.9 us
    dot_general x1, matrix products, per_device(): jnp.dot(hidden, down_matrix, preferred_element_type=jnp.float32)  13.1 us
    another operation x1, local copies, waits for them, and re-layouts, per_device(): jnp.tile(value, repeats)  10.4 us
  transfers between devices with their start and end apart: 3, of which 3 were waited for; matrix products, arithmetic and copies ran while one was open for 1% of the time, Pallas kernels for 0%

profile of v1, /device:TPU:8, one launch (start us, length us, event | category | flops | bytes accessed | tf_op | source)
XLA Modules:
  0.0 307.6 jit_solution(10668469831146113696)
XLA Ops:
  6.5 0.0 copy-start
  6.5 0.8 copy.30
  7.3 0.1 eq.59
  7.4 0.1 fusion.9
  7.5 0.1 reduce_window_sum.11
  7.6 0.2 select_reduce_fusion
  7.8 0.1 reduce_sum.21
  7.9 0.1 copy.31
  8.0 0.7 multiply_add_fusion
  8.7 0.0 copy-done
  8.7 0.2 convolution_convert_fusion.1
  8.9 0.1 broadcast_in_dim.2
  8.9 34.1 %all_to_all.15 = bf16[32,16,768]{2,1,0:T(8,128)(2,1)} all-to-all(bf16[32,16,768]{2,1,0:T(8,128)(2,1)S(1)} %bitcast.37), channel_id=1, replica_groups=mesh['ep'=32,'tp'=8] {'ep'}, dimensions={0} | all-to-all | bytes 1572864 | tf_op jit(solution)/shard_map/all_to_all | solution.py:53
  43.0 5.2 %copy.32 = bf16[32,16,768]{0,1,2:T(8,128)(2,1)S(1)} copy(bf16[32,16,768]{2,1,0:T(8,128)(2,1)} %all_to_all.15) | data formatting | bytes 1572864 | tf_op jit(solution)/shard_map/all_to_all | solution.py:53
  48.2 10.4 %tile.4 = bf16[32,16,8,768]{0,1,3,2:T(8,128)(2,1)} broadcast(bf16[32,16,768]{0,1,2:T(8,128)(2,1)S(1)} %copy.32), dimensions={0,1,3} | broadcast | bytes 7077888 | tf_op jit(solution)/shard_map/tile | solution.py:59
  58.6 27.2 %reshape.50 = bf16[8,2,196608]{2,1,0:T(2,128)(2,1)} reshape(bf16[6144,16,32]{2,1,0:T(8,128)(2,1)} %bitcast.32) | data formatting | bytes 12582912
  85.8 0.0 copy-start.2
  85.8 0.0 copy-start.5
  85.8 5.1 %all-to-all-start.1 = ((bf16[8,2,196608]{2,1,0:T(2,128)(2,1)}), bf16[8,2,196608]{2,1,0:T(2,128)(2,1)}, u32[]{:S(2)}, u32[]{:S(2)}) async-start(bf16[8,2,196608]{2,1,0:T(2,128)(2,1)} %reshape.50), calls=%async_computation.1 | async-start | bytes 12582912 | tf_op jit(solution)/shard_map/all_to_all | solution.py:58
  90.8 0.0 copy-start.6
  90.8 0.2 reduce-scatter.2.cloned.1.call-start
  91.1 0.0 copy-done.2
  91.1 0.0 copy-done.5
  91.1 0.0 copy-start.3
  91.1 1.9 bitcast_multiply_fusion.2
  93.0 0.0 copy-done.6
  93.0 1.1 copy-done.3
  94.1 0.0 copy-start.4
  94.1 0.0 copy-start.7
  94.1 0.3 bitcast_multiply_fusion
  94.4 1.6 copy-done.4
  96.0 0.0 copy-done.7
  96.0 1.9 bitcast_multiply_fusion.1
  97.9 65.1 %all-to-all-done.1 = bf16[8,2,196608]{2,1,0:T(2,128)(2,1)} async-done(((bf16[8,2,196608]{2,1,0:T(2,128)(2,1)}), bf16[8,2,196608]{2,1,0:T(2,128)(2,1)}, u32[]{:S(2)}, u32[]{:S(2)}) %all-to-all-start.1) | async-done | bytes 6291488 | tf_op jit(solution)/shard_map/all_to_all | solution.py:58
  162.9 16.3 %reshape.51 = bf16[6144,16,32]{2,1,0:T(8,128)(2,1)} reshape(bf16[8,2,196608]{2,1,0:T(2,128)(2,1)} %all-to-all-done.1) | data formatting | bytes 12582912
  179.3 28.9 %copy.33 = bf16[32,16,6144]{2,1,0:T(8,128)(2,1)} copy(bf16[32,16,6144]{0,1,2:T(8,128)(2,1)} %bitcast.33) | data formatting | bytes 12582912 | tf_op jit(solution)/shard_map/all_to_all | solution.py:58
  208.2 6.3 %fusion.20 = f32[512,256]{1,0:T(8,128)} fusion(bf16[512,6144]{1,0:T(8,128)(2,1)} %bitcast.35, bf16[6144,256]{1,0:T(8,128)(2,1)} %bitcast_multiply_fusion.2), kind=kOutput, calls=%fused_computation.40 | convolution fusion | flops 1610612736 | bytes 9961472 | tf_op jit(solution)/shard_map/dot_general | solution.py:63
  214.5 13.1 %convolution_convert_fusion = bf16[512,6144]{1,0:T(8,128)(2,1)} fusion(bf16[256,6144]{1,0:T(8,128)(2,1)S(1)} %bitcast_multiply_fusion, bf16[512,6144]{1,0:T(8,128)(2,1)} %bitcast.36, bf16[6144,256]{1,0:T(8,128)(2,1)} %bitcast_multiply_fusion.1, f32[512,256]{1,0:T(8,128)} %fusion.20), kind=kOutput, calls=%fused_computation | convolution fusion | flops 3225157632 | bytes 19398656 | tf_op jit(solution)/shard_map/dot_general | solution.py:66
  227.6 0.0 copy-start.1
  227.6 0.0 copy-start.8
  227.6 0.0 reduce-scatter.2.cloned.1.call-update
  227.6 40.1 %reduce-scatter.2.cloned.1.call-done = bf16[32,16,768]{2,1,0:T(8,128)(2,1)} async-done(((bf16[32,16,6144]{2,1,0:T(8,128)(2,1)}), bf16[32,16,768]{2,1,0:T(8,128)(2,1)}) %reduce-scatter.2.cloned.1.call-update) | async-done | bytes 786448 | tf_op jit(solution)/shard_map/reduce_scatter | solution.py:70
  267.7 10.2 %all-to-all-start.2 = ((bf16[32,16,768]{2,1,0:T(8,128)(2,1)}), bf16[32,16,768]{2,1,0:T(8,128)(2,1)S(1)}, u32[]{:S(2)}, u32[]{:S(2)}) async-start(bf16[32,16,768]{2,1,0:T(8,128)(2,1)} %reduce-scatter.2.cloned.1.call-done), calls=%async_computation.3 | async-start | bytes 1572864 | tf_op jit(solution)/shard_map/all_to_all | solution.py:76
  277.8 0.0 copy-done.8
  277.9 21.9 %all-to-all-done.2 = bf16[32,16,768]{2,1,0:T(8,128)(2,1)S(1)} async-done(((bf16[32,16,768]{2,1,0:T(8,128)(2,1)}), bf16[32,16,768]{2,1,0:T(8,128)(2,1)S(1)}, u32[]{:S(2)}, u32[]{:S(2)}) %all-to-all-start.2) | async-done | bytes 786464 | tf_op jit(solution)/shard_map/all_to_all | solution.py:76
  299.8 0.1 convert_reduce_fusion
  299.9 0.8 convolution_convert_fusion.2
  300.7 0.0 copy-done.1
  (2 shorter events, 0.0 us)
Async XLA Ops:
  6.5 2.1 copy-start
  85.8 5.3 %copy-start.2 = (bf16[6144,256]{1,0:T(8,128)(2,1)S(1)}, bf16[6144,256]{1,0:T(8,128)(2,1)}, u32[]{:S(2)}) copy-start(bf16[6144,256]{1,0:T(8,128)(2,1)} %param.12) | copy-start | bytes 9437188
  85.8 5.3 %copy-start.5 = (bf16[192,256]{1,0:T(8,128)(2,1)S(1)}, bf16[192,256]{1,0:T(8,128)(2,1)}, u32[]{:S(2)}) copy-start(bf16[192,256]{1,0:T(8,128)(2,1)} %param.13) | copy-start | bytes 294916
  85.8 77.2 %all-to-all-start.1 = ((bf16[8,2,196608]{2,1,0:T(2,128)(2,1)}), bf16[8,2,196608]{2,1,0:T(2,128)(2,1)}, u32[]{:S(2)}, u32[]{:S(2)}) async-start(bf16[8,2,196608]{2,1,0:T(2,128)(2,1)} %reshape.50), calls=%async_computation.1 | async-start | bytes 12582912 | tf_op jit(solution)/shard_map/all_to_all | solution.py:58
  90.8 2.2 copy-start.6
  90.8 176.8 %reduce-scatter.2.cloned.1.call-start = ((), (), s32[]{:S(2)}) async-start(), calls=%async_computation.4 | async-start | bytes 7077888 | tf_op jit(solution)/shard_map/reduce_scatter | solution.py:70
  91.1 3.0 copy-start.3
  94.1 1.9 copy-start.4
  94.1 1.9 copy-start.7
  227.6 73.1 %copy-start.1 = (bf16[32,768]{1,0:T(8,128)(2,1)S(1)}, bf16[32,768]{1,0:T(8,128)(2,1)}, u32[]{:S(2)}) copy-start(bf16[32,768]{1,0:T(8,128)(2,1)} %param.9) | copy-start | bytes 147460
  227.6 50.3 %copy-start.8 = (f32[32,2]{0,1:T(2,128)S(1)}, f32[32,2]{0,1:T(2,128)}, u32[]{:S(2)}) copy-start(f32[32,2]{0,1:T(2,128)} %param.11) | copy-start | bytes 772
  267.7 32.1 %all-to-all-start.2 = ((bf16[32,16,768]{2,1,0:T(8,128)(2,1)}), bf16[32,16,768]{2,1,0:T(8,128)(2,1)S(1)}, u32[]{:S(2)}, u32[]{:S(2)}) async-start(bf16[32,16,768]{2,1,0:T(8,128)(2,1)} %reduce-scatter.2.cloned.1.call-done), calls=%async_computation.3 | async-start | bytes 1572864 | tf_op jit(solution)/shard_map/all_to_all | solution.py:76
Sparse Core Ops, SparseCore 0:
  227.7 39.8 reduce-scatter.1
